TPU v7x, 256 devices: a whole 4x4x8 slice. The times are simulated.
256 devices in a mesh: rows: 128 (over x, y_hi, z, core), cols: 2 (over y_lo).
Axes of the slice: x: 4, y: 4 (y_hi: 2, y_lo: 2; y = y_hi * 2 + y_lo), z: 8, core: 2. Of those that a mesh axis runs over, the one named last changes fastest.
Arguments:
- ancestor: bfloat16 [24576, 24576], P('rows', 'cols'), may hold values from -6 to 6
- panel_below: bfloat16 [2048, 512], P('rows'), may hold values from -0.0625 to 0.0625
- panel_beside: bfloat16 [2048, 512], P('rows'), may hold values from -0.0625 to 0.0625
- inverse_lower: bfloat16 [512, 512], replicated, may hold values from -3 to 3
- inverse_upper: bfloat16 [512, 512], replicated, may hold values from -3 to 3
- list_below: int32 [16], replicated, may hold values from 0 to 191, as said below
- list_beside: int32 [16], replicated, may hold values from 0 to 191, as said below
- second_below: bfloat16 [2048, 512], P('rows'), may hold values from -0.0625 to 0.0625
- second_beside: bfloat16 [2048, 512], P('rows'), may hold values from -0.0625 to 0.0625
- linked_below: bfloat16 [512, 512], replicated, may hold values from -0.0625 to 0.0625
- linked_beside: bfloat16 [512, 512], replicated, may hold values from -0.0625 to 0.0625
- second_lower: bfloat16 [512, 512], replicated, may hold values from -3 to 3
- second_upper: bfloat16 [512, 512], replicated, may hold values from -3 to 3
- blocks_below: int32 [16], replicated, may hold values from 0 to 191, as said below
- blocks_beside: int32 [16], replicated, may hold values from 0 to 191, as said below
Outputs:
- new_lower: bfloat16 [24576, 512], P('rows', 'cols')
- new_upper: bfloat16 [24576, 512], P(('cols', 'rows'))
- new_diagonal: bfloat16 [512, 512], P(None, 'cols')
- next_lower: bfloat16 [24576, 512], P('rows', 'cols')
- next_upper: bfloat16 [24576, 512], P(('cols', 'rows'))
- next_link: bfloat16 [512, 512], replicated
- next_diagonal: bfloat16 [512, 512], P(None, 'cols')
Inputs may be any that keep to these rules, and one draw needn't show every extreme that they name: `list_below`: 16 distinct block numbers in ascending order; block 0 and block 191 are always listed. `list_beside`: 16 distinct block numbers in ascending order; block 0 and block 191 are always listed. `blocks_below`: 16 distinct block numbers in ascending order; block 0 and block 191 are always listed. `blocks_beside`: 16 distinct block numbers in ascending order; block 0 and block 191 are always listed.
All inputs are finite; a program needn't handle non-finite values.
Results may differ from a plain program's by a relative error of at most 0.0077.
Values may be sent and summed in bfloat16 or wider, within the bound.
A program may use at most 128 MiB of HBM per device.

v0:
```python
import jax
import jax.numpy as jnp
from jax import lax
from jax.sharding import PartitionSpec as P

BLK = 128


def normalise(panel, inverse):
    return jnp.dot(panel, inverse, preferred_element_type=jnp.float32).astype(jnp.bfloat16)


def normalise_by_rows(panel, inverse):
    return lax.dot_general(
        panel, inverse, (((1,), (1,)), ((), ())), preferred_element_type=jnp.float32
    ).astype(jnp.bfloat16)


def inner_rows(left, right):
    return lax.dot_general(
        left, right, (((0,), (0,)), ((), ())), preferred_element_type=jnp.float32
    )


def own_half(panel, first_column, half_width):
    return lax.dynamic_slice_in_dim(panel, first_column, half_width, 1)


def listed_columns(tile, blocks, first_block):
    block_count = tile.shape[1] // BLK
    local_ids = blocks - first_block
    inside = jnp.logical_and(local_ids >= 0, local_ids < block_count)
    picked = jnp.take(
        tile.reshape(tile.shape[0], block_count, BLK),
        jnp.clip(local_ids, 0, block_count - 1),
        axis=1,
    )
    return (picked.reshape(tile.shape[0], blocks.shape[0] * BLK), jnp.repeat(inside, BLK))


def masked_product(picked, inside, panel):
    kept = jnp.where(inside[:, None], panel, jnp.zeros_like(panel))
    return jnp.dot(picked, kept, preferred_element_type=jnp.float32)


def listed_rows(strips, blocks):
    shaped = strips.reshape(strips.shape[0] // BLK, BLK, strips.shape[1])
    return jnp.take(shaped, blocks, axis=0).reshape(blocks.shape[0] * BLK, strips.shape[1])


def rows_onto(panel, blocks, first_row, row_count):
    global_rows = first_row + jnp.arange(row_count, dtype=jnp.int32)
    block_of = global_rows // BLK
    offset = global_rows % BLK
    matches = block_of[:, None] == blocks[None, :]
    position = jnp.sum(
        jnp.where(matches, jnp.arange(blocks.shape[0], dtype=jnp.int32)[None, :], 0), axis=1
    )
    present = jnp.any(matches, axis=1)
    picked = jnp.take(panel, position * BLK + offset, axis=0)
    return jnp.where(present[:, None], picked, jnp.zeros_like(picked))


def lower_block(partial_value):
    return (-lax.psum_scatter(partial_value, "cols", scatter_dimension=1, tiled=True)).astype(
        jnp.bfloat16
    )


def diag_block(base_value, picked_rows, lower_local):
    summed = lax.psum(inner_rows(picked_rows, lower_local), "rows")
    return (base_value - summed).astype(jnp.bfloat16)


def body(
    ancestor,
    panel_below,
    panel_beside,
    inverse_lower,
    inverse_upper,
    list_below,
    list_beside,
    second_below,
    second_beside,
    linked_below,
    linked_beside,
    second_lower,
    second_upper,
    blocks_below,
    blocks_beside,
):
    row_devices = lax.axis_size("rows")
    row_at = lax.axis_index("rows")
    col_at = lax.axis_index("cols")
    col_devices = lax.axis_size("cols")
    tile_rows = ancestor.shape[0]
    tile_cols = ancestor.shape[1]
    width = inverse_lower.shape[0]
    half_width = width // col_devices
    first_column = col_at * half_width
    unit_below = normalise(panel_below, inverse_lower)
    unit_beside = normalise_by_rows(panel_beside, inverse_upper)
    below_next = normalise(second_below, second_lower)
    beside_next = normalise_by_rows(second_beside, second_upper)
    unit_below, unit_beside, below_next, beside_next = (
        lax.all_gather(unit_below, "rows", axis=0, tiled=True),
        lax.all_gather(unit_beside, "rows", axis=0, tiled=True),
        lax.all_gather(below_next, "rows", axis=0, tiled=True),
        lax.all_gather(beside_next, "rows", axis=0, tiled=True),
    )
    strips = lax.all_to_all(ancestor, "rows", split_axis=1, concat_axis=0, tiled=True)
    strip_width = tile_cols // row_devices
    strip_start = (col_at * row_devices + row_at) * strip_width
    first_block = col_at * (tile_cols // BLK)
    row_start = row_at * tile_rows
    picked, inside = listed_columns(ancestor, list_below, first_block)
    new_lower = lower_block(masked_product(picked, inside, unit_below))
    new_upper = (-inner_rows(listed_rows(strips, list_beside), unit_beside)).astype(jnp.bfloat16)
    base_first = jnp.dot(
        inverse_upper,
        own_half(inverse_lower, first_column, half_width),
        preferred_element_type=jnp.float32,
    )
    new_diagonal = diag_block(
        base_first, rows_onto(unit_beside, list_beside, row_start, tile_rows), new_lower
    )
    link_below = normalise(linked_below, second_lower)
    link_beside = normalise_by_rows(linked_beside, second_upper)
    link_rows = lax.dynamic_slice_in_dim(link_below, first_column, half_width, 0)
    picked_next, inside_next = listed_columns(ancestor, blocks_below, first_block)
    partial_value = masked_product(picked_next, inside_next, below_next) + jnp.dot(
        new_lower, link_rows, preferred_element_type=jnp.float32
    )
    next_lower = lower_block(partial_value)
    first_row = (row_at == 0).astype(jnp.float32)
    link_term = inner_rows(
        new_upper, rows_onto(below_next, blocks_below, strip_start, strip_width)
    ) + first_row * jnp.dot(new_diagonal, link_rows, preferred_element_type=jnp.float32)
    next_link = (-lax.psum(link_term, ("rows", "cols"))).astype(jnp.bfloat16)
    next_upper = (
        -(
            inner_rows(listed_rows(strips, blocks_beside), beside_next)
            + jnp.dot(new_upper, link_beside, preferred_element_type=jnp.float32)
        )
    ).astype(jnp.bfloat16)
    base_second = jnp.dot(
        second_upper,
        own_half(second_lower, first_column, half_width),
        preferred_element_type=jnp.float32,
    ) - inner_rows(link_beside, own_half(next_link, first_column, half_width))
    next_diagonal = diag_block(
        base_second, rows_onto(beside_next, blocks_beside, row_start, tile_rows), next_lower
    )
    return (new_lower, new_upper, new_diagonal, next_lower, next_upper, next_link, next_diagonal)


def solution(mesh):
    return jax.shard_map(
        body,
        mesh=mesh,
        in_specs=(
            P("rows", "cols"),
            P("rows", None),
            P("rows", None),
            P(),
            P(),
            P(),
            P(),
            P("rows", None),
            P("rows", None),
            P(),
            P(),
            P(),
            P(),
            P(),
            P(),
        ),
        out_specs=(
            P("rows", "cols"),
            P(("cols", "rows"), None),
            P(None, "cols"),
            P("rows", "cols"),
            P(("cols", "rows"), None),
            P(),
            P(None, "cols"),
        ),
        check_vma=False,
    )
```

profile of v0, /device:TPU:2, one launch (start us, length us, event | category | flops | bytes accessed | tf_op | source)
XLA Modules:
  0.0 2101.3 jit_solution(3499471611282957993)
XLA Ops:
  7.2 1.9 convolution_convert_fusion.4
  9.2 1.5 convolution_convert_fusion.2
  11.5 5.8 copy_bitcast_fusion
  17.3 3.0 gather_fusion.1
  20.4 110.8 %all-gather.5.cloned.1.call-done = bf16[2048,512]{1,0:T(8,128)(2,1)} async-done(((bf16[16,512]{1,0:T(8,128)(2,1)}), bf16[2048,512]{1,0:T(8,128)(2,1)}) %all-gather.5.cloned.1.call-update) | async-done | bytes 2097168 | tf_op jit(solution)/shard_map/all_gather | solution.py:106
  131.3 3.1 fusion.2
  135.3 10.1 all_to_all.12
  145.3 9.5 copy.76
  154.8 9.5 all-to-all-start
  165.4 3.0 gather_fusion.4
  169.3 86.8 %all-gather.9.cloned.1.call-done = bf16[2048,512]{1,0:T(8,128)(2,1)} async-done(((bf16[16,512]{1,0:T(8,128)(2,1)}), bf16[2048,512]{1,0:T(8,128)(2,1)}) %all-gather.9.cloned.1.call-update) | async-done | bytes 2097168 | tf_op jit(solution)/shard_map/all_gather | solution.py:108
  256.1 2.2 fusion
  258.3 20.8 reduce-scatter.3.cloned.1.call-done
  281.6 120.8 %all-gather.11.cloned.1.call-done = bf16[2048,512]{1,0:T(8,128)(2,1)} async-done(((bf16[16,512]{1,0:T(8,128)(2,1)}), bf16[2048,512]{1,0:T(8,128)(2,1)}) %all-gather.11.cloned.1.call-update) | async-done | bytes 2097168 | tf_op jit(solution)/shard_map/all_gather | solution.py:109
  402.4 2.9 gather_fusion.6
  405.3 114.1 %all-gather.7.cloned.1.call-done = bf16[2048,512]{1,0:T(8,128)(2,1)} async-done(((bf16[16,512]{1,0:T(8,128)(2,1)}), bf16[2048,512]{1,0:T(8,128)(2,1)}) %all-gather.7.cloned.1.call-update) | async-done | bytes 2097168 | tf_op jit(solution)/shard_map/all_gather | solution.py:107
  519.4 2.9 gather_fusion.3
  523.5 13.4 reduce-scatter.5.cloned.1.call-done
  538.5 1.1 fusion.29
  540.8 1.5 convolution_convert_fusion
  542.3 3.3 gather_fusion
  545.6 1206.7 %all-reduce.6.cloned.1.call-done = (f32[512,256]{0,1:T(8,128)}, f32[512,256]{0,1:T(8,128)}) async-done(((f32[512,256]{0,1:T(8,128)}, f32[512,256]{0,1:T(8,128)}), (f32[512,256]{0,1:T(8,128)}, f32[512,256]{0,1:T(8,128)})) %all-reduce.6.cloned.1.call-update) | async-done | bytes 1048592 | tf_op jit(solution)/shard_map/psum | solution.py:71
  1752.3 1.4 fusion.10
  1754.6 1.3 convolution_multiply_fusion
  1755.9 8.2 copy.78
  1764.1 3.0 gather_fusion.2
  1767.1 1.3 fusion.12
  1769.0 1.3 convolution_add_fusion
  1770.4 3.0 gather_fusion.5
  1775.1 315.4 %all-reduce.4.cloned.1.call-done = f32[512,512]{1,0:T(8,128)} async-done(((f32[512,512]{1,0:T(8,128)}), f32[512,512]{1,0:T(8,128)}) %all-reduce.4.cloned.1.call-update) | async-done | bytes 1048592 | tf_op jit(solution)/shard_map/psum | solution.py:139
  2090.5 1.3 negate_convert_fusion
  2092.2 1.4 fusion.9
  (94 shorter events, 14.3 us)
Async XLA Ops:
  7.2 2.0 copy-start
  7.2 124.1 %all-gather.5.cloned.1.call-start = ((), (), s32[]{:S(2)}) async-start(), calls=%async_computation.3 | async-start | bytes 2113536 | tf_op jit(solution)/shard_map/all_gather | solution.py:106
  9.2 246.9 %all-gather.9.cloned.1.call-start = ((), (), s32[]{:S(2)}) async-start(), calls=%async_computation.6 | async-start | bytes 2113536 | tf_op jit(solution)/shard_map/all_gather | solution.py:108
  10.7 268.4 %reduce-scatter.3.cloned.1.call-start = ((), (), s32[]{:S(2)}) async-start(), calls=%async_computation.4 | async-start | bytes 589824 | tf_op jit(solution)/shard_map/reduce_scatter | solution.py:65
  131.2 3.1 copy-start.2
  131.2 3.1 copy-start.15
  134.3 268.1 %all-gather.11.cloned.1.call-start = ((), (), s32[]{:S(2)}) async-start(), calls=%async_computation.8 | async-start | bytes 2113536 | tf_op jit(solution)/shard_map/all_gather | solution.py:109
  154.8 9.6 copy-start.5
  154.8 9.6 copy-start.16
  154.8 1601.1 %all-to-all-start = ((bf16[192,128,96]{2,0,1:T(8,128)(2,1)}), bf16[192,128,96]{2,0,1:T(8,128)(2,1)}, u32[]{:S(2)}, u32[]{:S(2)}) async-start(bf16[192,128,96]{2,0,1:T(8,128)(2,1)} %copy.76), calls=%async_computation.1 | async-start | bytes 12582912 | tf_op jit(solution)/shard_map/all_to_all | solution.py:111
  164.3 4.2 copy-start.17
  164.3 4.2 copy-start.18
  164.3 4.3 copy-start.19
  164.3 4.5 copy-start.10
  164.3 355.1 %all-gather.7.cloned.1.call-start = ((), (), s32[]{:S(2)}) async-start(), calls=%async_computation.5 | async-start | bytes 2113536 | tf_op jit(solution)/shard_map/all_gather | solution.py:107
  165.3 371.6 %reduce-scatter.5.cloned.1.call-start = ((), (), s32[]{:S(2)}) async-start(), calls=%async_computation.7 | async-start | bytes 589824 | tf_op jit(solution)/shard_map/reduce_scatter | solution.py:65
  280.1 242.2 %copy-start.9 = (bf16[192,256]{1,0:T(8,128)(2,1)}, bf16[192,256]{1,0:T(8,128)(2,1)S(1)}, u32[]{:S(2)}) copy-start(bf16[192,256]{1,0:T(8,128)(2,1)S(1)} %negate_convert_fusion.2) | copy-start | bytes 294916
  281.1 1471.2 %all-reduce.6.cloned.1.call-start = ((), (), s32[]{:S(2)}) async-start(), calls=%async_computation.10 | async-start | bytes 2097152 | tf_op jit(solution)/shard_map/psum | solution.py:71
  537.8 0.6 copy-start.14
  538.5 1213.9 %copy-start.8 = (bf16[512,512]{1,0:T(8,128)(2,1)S(1)}, bf16[512,512]{1,0:T(8,128)(2,1)}, u32[]{:S(2)}) copy-start(bf16[512,512]{1,0:T(8,128)(2,1)} %param.24) | copy-start | bytes 1572868
  539.7 1550.8 %all-reduce.4.cloned.1.call-start = ((), (), s32[]{:S(2)}) async-start(), calls=%async_computation.9 | async-start | bytes 2097152 | tf_op jit(solution)/shard_map/psum | solution.py:139
  1755.9 11.2 copy-start.7
  1767.1 1.9 copy-start.4
  1767.1 1.9 copy-start.13
  1767.1 1.9 copy-start.20
  1768.4 0.6 copy-start.11
  1769.0 4.3 copy-start.1
  1773.4 0.9 copy-start.12
  1774.3 318.0 %copy-start.3 = (bf16[512,512]{1,0:T(8,128)(2,1)S(1)}, bf16[512,512]{1,0:T(8,128)(2,1)}, u32[]{:S(2)}) copy-start(bf16[512,512]{1,0:T(8,128)(2,1)} %param.33) | copy-start | bytes 1572868
  2091.8 2.6 copy-start.6
Sparse Core Ops, SparseCore 0:
  12.3 118.9 all-gather.4
  135.5 120.4 all-gather.8
  259.2 19.9 reduce-scatter.2
  283.3 119.0 all-gather.10
  406.5 112.8 all-gather.6
  521.7 15.1 reduce-scatter.4
  540.1 1212.1 all-reduce.5
  1770.5 319.9 all-reduce.3
where the time goes:
time: 2100 us
  waiting for transfers between devices  1990 us (95%)
  local copies, waits for them, and re-layouts  58.2 us (3%)
  matrix products  24.1 us (1%)
    psum x1, waiting for transfers between devices, diag_block(): summed = lax.psum(inner_rows(picked_rows, lower_local), 'rows')  1210 us
    psum x1, waiting for transfers between devices, body(): next_link = (-lax.psum(link_term, ('rows', 'cols'))).astype(jnp.bfloat16)  315 us
    all_gather x1, waiting for transfers between devices, body(): lax.all_gather(beside_next, 'rows', axis=0, tiled=True)  121 us
    all_gather x1, waiting for transfers between devices, body(): lax.all_gather(unit_beside, 'rows', axis=0, tiled=True)  114 us
    all_gather x1, waiting for transfers between devices, body(): lax.all_gather(unit_below, 'rows', axis=0, tiled=True)  111 us
    all_gather x1, waiting for transfers between devices, body(): lax.all_gather(below_next, 'rows', axis=0, tiled=True)  86.8 us
  transfers between devices with their start and end apart: 9, of which 8 were waited for; matrix products, arithmetic and copies ran while one was open for 3% of the time, Pallas kernels for 0%

commit v1 on v0

--- a/solution.py
+++ b/solution.py
@@ -68,7 +68,7 @@
 
 
 def diag_block(base_value, picked_rows, lower_local):
-    summed = lax.psum(inner_rows(picked_rows, lower_local), "rows")
+    summed = jnp.sum(lax.all_gather(inner_rows(picked_rows, lower_local), "rows"), axis=0)
     return (base_value - summed).astype(jnp.bfloat16)
 
 

time: 2100 us -> 1500 us (0.71)
  waiting for transfers between devices: 1990 us -> 1340 us
  other arithmetic: 5.43 us -> 46.3 us
    psum x1 -> x0, waiting for transfers between devices: 1210 us -> none  [diag_block(): summed = lax.psum(inner_rows(picked_rows, lower_local), 'rows')]
    all_gather x0 -> x2, waiting for transfers between devices: none -> 592 us  [diag_block(): lax.all_gather(inner_rows(picked_rows, lower_local), 'rows')]
    psum x1, waiting for transfers between devices: 315 us -> 255 us  [body(): next_link = (-lax.psum(link_term, ('rows', 'cols'))).astype(jnp.bfloat16)]
    all_to_all x1, waiting for transfers between devices: 0.01 us -> 59.9 us  [body(): lax.all_to_all(ancestor, 'rows', split_axis=1, concat_axis=0, tiled=True)]
    reduce_sum x0 -> x2, other arithmetic: none -> 41.9 us  [diag_block(): jnp.sum(lax.all_gather(inner_rows(picked_rows, lower_local), 'rows'), axi...]
    all_gather x1, waiting for transfers between devices: 121 us -> 93.3 us  [body(): lax.all_gather(beside_next, 'rows', axis=0, tiled=True)]
  transfers between devices with their start and end apart: 9 -> 10, of which waited for: 8 -> 10; matrix products, arithmetic and copies ran while one was open for 3% -> 6% of each run, Pallas kernels for 0% -> 0%
where the time goes in v1:
time: 1500 us
  waiting for transfers between devices  1340 us (89%)
  local copies, waits for them, and re-layouts  57.7 us (4%)
  other arithmetic  46.3 us (3%)
  matrix products  23.4 us (2%)
    all_gather x2, waiting for transfers between devices, diag_block(): lax.all_gather(inner_rows(picked_rows, lower_local), 'rows')  592 us
    psum x1, waiting for transfers between devices, body(): next_link = (-lax.psum(link_term, ('rows', 'cols'))).astype(jnp.bfloat16)  255 us
    all_gather x1, waiting for transfers between devices, body(): lax.all_gather(unit_beside, 'rows', axis=0, tiled=True)  113 us
    all_gather x1, waiting for transfers between devices, body(): lax.all_gather(unit_below, 'rows', axis=0, tiled=True)  110 us
    all_gather x1, waiting for transfers between devices, body(): lax.all_gather(beside_next, 'rows', axis=0, tiled=True)  93.3 us
    all_gather x1, waiting for transfers between devices, body(): lax.all_gather(below_next, 'rows', axis=0, tiled=True)  86.8 us
    all_to_all x1, waiting for transfers between devices, body(): lax.all_to_all(ancestor, 'rows', split_axis=1, concat_axis=0, tiled=True)  59.9 us
    reduce_sum x2, other arithmetic, diag_block(): jnp.sum(lax.all_gather(inner_rows(picked_rows, lower_local), 'rows'), axi...  41.9 us
  transfers between devices with their start and end apart: 10, of which 10 were waited for; matrix products, arithmetic and copies ran while one was open for 6% of the time, Pallas kernels for 0%

profile of v1, /device:TPU:2, one launch (start us, length us, event | category | flops | bytes accessed | tf_op | source)
XLA Modules:
  0.0 1496.3 jit_solution(17057768629103593012)
XLA Ops:
  7.2 1.9 convolution_convert_fusion.4
  9.2 1.9 convolution_convert_fusion.3
  11.9 5.9 copy_bitcast_fusion
  17.7 3.0 gather_fusion.1
  20.8 110.4 %all-gather.9.cloned.1.call-done = bf16[2048,512]{1,0:T(8,128)(2,1)} async-done(((bf16[16,512]{1,0:T(8,128)(2,1)}), bf16[2048,512]{1,0:T(8,128)(2,1)}) %all-gather.9.cloned.1.call-update) | async-done | bytes 2097168 | tf_op jit(solution)/shard_map/all_gather | solution.py:106
  131.3 3.0 fusion.2
  135.5 112.9 %all-gather.11.cloned.1.call-done = bf16[2048,512]{1,0:T(8,128)(2,1)} async-done(((bf16[16,512]{1,0:T(8,128)(2,1)}), bf16[2048,512]{1,0:T(8,128)(2,1)}) %all-gather.11.cloned.1.call-update) | async-done | bytes 2097168 | tf_op jit(solution)/shard_map/all_gather | solution.py:107
  248.4 2.9 gather_fusion.3
  251.3 15.3 %reduce-scatter.3.cloned.1.call-done = f32[192,256]{1,0:T(8,128)} async-done(((f32[192,512]{1,0:T(8,128)}), f32[192,256]{1,0:T(8,128)}) %reduce-scatter.3.cloned.1.call-update) | async-done | bytes 196624 | tf_op jit(solution)/shard_map/reduce_scatter | solution.py:65
  268.8 10.1 all_to_all.12
  278.8 9.4 copy.68
  288.3 14.1 all-to-all-start
  303.7 3.0 gather_fusion.4
  307.5 86.8 %all-gather.13.cloned.1.call-done = bf16[2048,512]{1,0:T(8,128)(2,1)} async-done(((bf16[16,512]{1,0:T(8,128)(2,1)}), bf16[2048,512]{1,0:T(8,128)(2,1)}) %all-gather.13.cloned.1.call-update) | async-done | bytes 2097168 | tf_op jit(solution)/shard_map/all_gather | solution.py:108
  394.3 3.3 gather_fusion
  397.6 2.2 fusion
  400.9 59.9 %all-to-all-done = bf16[192,128,96]{2,0,1:T(8,128)(2,1)} async-done(((bf16[192,128,96]{2,0,1:T(8,128)(2,1)}), bf16[192,128,96]{2,0,1:T(8,128)(2,1)}, u32[]{:S(2)}, u32[]{:S(2)}) %all-to-all-start) | async-done | bytes 4718624 | tf_op jit(solution)/shard_map/all_to_all | solution.py:111
  460.8 8.0 copy.70
  468.8 3.0 gather_fusion.2
  471.8 2.1 fusion.12
  474.0 266.3 %all-gather.17.cloned.1.call-done = f32[65536,256]{1,0:T(8,128)} async-done(((f32[512,256]{1,0:T(8,128)}), f32[65536,256]{1,0:T(8,128)}) %all-gather.17.cloned.1.call-update) | async-done | bytes 67108880 | tf_op jit(solution)/shard_map/all_gather | solution.py:71
  740.2 21.0 %reduce_sum.46 = f32[512,256]{1,0:T(8,128)S(1)} reduce(f32[128,512,256]{2,1,0:T(8,128)} %bitcast.5, f32[]{:T(128)} %constant.124.clone.1), dimensions={0}, to_apply=%region_3.7 | reduce | flops 16646144 | bytes 67633152 | tf_op jit(solution)/shard_map/reduce_sum | solution.py:71
  762.3 1.4 convolution_add_fusion
  763.8 93.3 %all-gather.15.cloned.1.call-done = bf16[2048,512]{1,0:T(8,128)(2,1)} async-done(((bf16[16,512]{1,0:T(8,128)(2,1)}), bf16[2048,512]{1,0:T(8,128)(2,1)}) %all-gather.15.cloned.1.call-update) | async-done | bytes 2097168 | tf_op jit(solution)/shard_map/all_gather | solution.py:109
  857.1 2.9 gather_fusion.6
  860.0 14.7 reduce-scatter.5.cloned.1.call-done
  876.9 1.7 convolution_convert_fusion
  878.6 3.7 gather_fusion.5
  882.3 1.5 fusion.20
  885.5 254.5 %all-reduce.2.cloned.1.call-done = f32[512,512]{1,0:T(8,128)} async-done(((f32[512,512]{1,0:T(8,128)}), f32[512,512]{1,0:T(8,128)}) %all-reduce.2.cloned.1.call-update) | async-done | bytes 1048592 | tf_op jit(solution)/shard_map/psum | solution.py:139
  1141.7 325.7 %all-gather.19.cloned.1.call-done = f32[65536,256]{1,0:T(8,128)} async-done(((f32[512,256]{1,0:T(8,128)}), f32[65536,256]{1,0:T(8,128)}) %all-gather.19.cloned.1.call-update) | async-done | bytes 67108880 | tf_op jit(solution)/shard_map/all_gather | solution.py:71
  1467.4 20.9 %reduce_sum.49 = f32[512,256]{1,0:T(8,128)S(1)} reduce(f32[128,512,256]{2,1,0:T(8,128)} %bitcast.12, f32[]{:T(128)} %constant.124.clone.1), dimensions={0}, to_apply=%region_10.14 | reduce | flops 16646144 | bytes 67633152 | tf_op jit(solution)/shard_map/reduce_sum | solution.py:71
  (94 shorter events, 15.3 us)
Async XLA Ops:
  7.2 127.2 %copy-start = (bf16[512,512]{1,0:T(8,128)(2,1)S(1)}, bf16[512,512]{1,0:T(8,128)(2,1)}, u32[]{:S(2)}) copy-start(bf16[512,512]{1,0:T(8,128)(2,1)} %param.32) | copy-start | bytes 1572868
  7.2 124.1 %all-gather.9.cloned.1.call-start = ((), (), s32[]{:S(2)}) async-start(), calls=%async_computation.3 | async-start | bytes 2113536 | tf_op jit(solution)/shard_map/all_gather | solution.py:106
  9.2 239.2 %all-gather.11.cloned.1.call-start = ((), (), s32[]{:S(2)}) async-start(), calls=%async_computation.5 | async-start | bytes 2113536 | tf_op jit(solution)/shard_map/all_gather | solution.py:107
  11.1 255.5 %reduce-scatter.3.cloned.1.call-start = ((), (), s32[]{:S(2)}) async-start(), calls=%async_computation.4 | async-start | bytes 589824 | tf_op jit(solution)/shard_map/reduce_scatter | solution.py:65
  131.2 3.1 copy-start.12
  131.2 4.0 copy-start.14
  131.3 4.0 copy-start.15
  134.3 260.0 %all-gather.13.cloned.1.call-start = ((), (), s32[]{:S(2)}) async-start(), calls=%async_computation.6 | async-start | bytes 2113536 | tf_op jit(solution)/shard_map/all_gather | solution.py:108
  135.2 605.0 %all-gather.17.cloned.1.call-start = ((), (), s32[]{:S(2)}) async-start(), calls=%async_computation.10 | async-start | bytes 67633152 | tf_op jit(solution)/shard_map/all_gather | solution.py:71
  267.6 132.3 %copy-start.10 = (bf16[192,256]{1,0:T(8,128)(2,1)}, bf16[192,256]{1,0:T(8,128)(2,1)S(1)}, u32[]{:S(2)}) copy-start(bf16[192,256]{1,0:T(8,128)(2,1)S(1)} %negate_convert_fusion.2) | copy-start | bytes 294916
  288.3 14.2 copy-start.2
  288.3 14.2 copy-start.13
  288.3 15.3 %copy-start.16 = (s32[16]{0:T(128)S(1)}, s32[16]{0:T(128)}, u32[]{:S(2)}) copy-start(s32[16]{0:T(128)} %param.34) | copy-start | bytes 196
  288.3 172.5 %all-to-all-start = ((bf16[192,128,96]{2,0,1:T(8,128)(2,1)}), bf16[192,128,96]{2,0,1:T(8,128)(2,1)}, u32[]{:S(2)}, u32[]{:S(2)}) async-start(bf16[192,128,96]{2,0,1:T(8,128)(2,1)} %copy.68), calls=%async_computation.1 | async-start | bytes 12582912 | tf_op jit(solution)/shard_map/all_to_all | solution.py:111
  302.4 4.7 copy-start.7
  302.4 554.6 %all-gather.15.cloned.1.call-start = ((), (), s32[]{:S(2)}) async-start(), calls=%async_computation.8 | async-start | bytes 2113536 | tf_op jit(solution)/shard_map/all_gather | solution.py:109
  303.4 571.3 %reduce-scatter.5.cloned.1.call-start = ((), (), s32[]{:S(2)}) async-start(), calls=%async_computation.7 | async-start | bytes 589824 | tf_op jit(solution)/shard_map/reduce_scatter | solution.py:65
  400.9 739.1 %all-reduce.2.cloned.1.call-start = ((), (), s32[]{:S(2)}) async-start(), calls=%async_computation.9 | async-start | bytes 2097152 | tf_op jit(solution)/shard_map/psum | solution.py:139
  473.9 409.8 %copy-start.8 = (bf16[96,512]{1,0:T(8,128)(2,1)}, bf16[96,512]{1,0:T(8,128)(2,1)S(1)}, u32[]{:S(2)}) copy-start(bf16[96,512]{1,0:T(8,128)(2,1)S(1)} %fusion.12) | copy-start | bytes 294916
  740.2 21.2 %copy-start.4 = (bf16[512,512]{1,0:T(8,128)(2,1)S(1)}, bf16[512,512]{1,0:T(8,128)(2,1)}, u32[]{:S(2)}) copy-start(bf16[512,512]{1,0:T(8,128)(2,1)} %param.25) | copy-start | bytes 1572868
  740.2 21.2 %copy-start.6 = (bf16[512,512]{1,0:T(8,128)(2,1)S(1)}, bf16[512,512]{1,0:T(8,128)(2,1)}, u32[]{:S(2)}) copy-start(bf16[512,512]{1,0:T(8,128)(2,1)} %param.24) | copy-start | bytes 1572868
  761.4 0.9 copy-start.9
  763.7 703.7 %all-gather.19.cloned.1.call-start = ((), (), s32[]{:S(2)}) async-start(), calls=%async_computation.11 | async-start | bytes 67633152 | tf_op jit(solution)/shard_map/all_gather | solution.py:71
  860.0 22.3 %copy-start.1 = (bf16[2048,512]{1,0:T(8,128)(2,1)S(1)}, bf16[2048,512]{1,0:T(8,128)(2,1)}, u32[]{:S(2)}) copy-start(bf16[2048,512]{1,0:T(8,128)(2,1)} %all-gather.15.cloned.1.call-done) | copy-start | bytes 6291460
  875.7 1.2 copy-start.11
  1141.4 326.1 %copy-start.5 = (bf16[512,512]{1,0:T(8,128)(2,1)}, bf16[512,512]{1,0:T(8,128)(2,1)S(1)}, u32[]{:S(2)}) copy-start(bf16[512,512]{1,0:T(8,128)(2,1)S(1)} %negate_convert_fusion) | copy-start | bytes 1572868
  1467.4 21.1 %copy-start.3 = (bf16[512,512]{1,0:T(8,128)(2,1)S(1)}, bf16[512,512]{1,0:T(8,128)(2,1)}, u32[]{:S(2)}) copy-start(bf16[512,512]{1,0:T(8,128)(2,1)} %param.33) | copy-start | bytes 1572868
Sparse Core Ops, SparseCore 0:
  12.3 118.9 all-gather.8
  135.5 112.8 all-gather.10
  251.5 15.1 reduce-scatter.2
  270.8 123.4 all-gather.12
  398.4 341.7 all-gather.16
  744.4 112.6 all-gather.14
  859.6 15.1 reduce-scatter.4
  880.2 259.8 all-reduce.1
  1143.7 323.6 all-gather.18
